TPU v7x, 32 devices: a whole 2x2x4 slice. The times are simulated.
32 devices in a mesh: dp: 8 (over z, core), row: 2 (over x), col: 2 (over y).
Axes of the slice: x: 2, y: 2, z: 4, core: 2. Of those that a mesh axis runs over, the one named last changes fastest.
Arguments:
- tokens: bfloat16 [16384, 1024], P(('dp', 'row'), 'col'), may hold values from -6 to 6
- mixer_gain: float32 [1024], P('col'), may hold values from 0.1 to 1.9
- in_weight: bfloat16 [1024, 3, 1024], P('col', None, 'row'), may hold values from -0.1875 to 0.1875
- conv_kernel: float32 [3, 1024], P(None, 'row'), may hold values from -3.5 to 3.5
- out_weight: bfloat16 [1024, 1024], P('row', 'col'), may hold values from -0.1875 to 0.1875
- ffn_gain: float32 [1024], P('col'), may hold values from 0.1 to 1.9
- ffn_weight: bfloat16 [1024, 2, 4608], P('col', None, 'row'), may hold values from -0.1875 to 0.1875
- down_weight: bfloat16 [4608, 1024], P('row', 'col'), may hold values from -0.1875 to 0.1875
- cotangent: bfloat16 [16384, 1024], P(('dp', 'row'), 'col'), may hold values from -6 to 6
Outputs:
- output: bfloat16 [16384, 1024], P(('dp', 'row'), 'col')
- d_tokens: float32 [16384, 1024], P(('dp', 'row'), 'col')
- d_mixer_gain: float32 [1024], P('col')
- d_in_weight: float32 [1024, 3, 1024], P('col', None, 'row')
- d_conv_kernel: float32 [3, 1024], P(None, 'row')
- d_out_weight: float32 [1024, 1024], P('row', 'col')
- d_ffn_gain: float32 [1024], P('col')
- d_ffn_weight: float32 [1024, 2, 4608], P('col', None, 'row')
- d_down_weight: float32 [4608, 1024], P('row', 'col')
All inputs are finite; a program needn't handle non-finite values.
Results may differ from a plain program's by a relative error of at most 0.015.
Values may be sent and summed in bfloat16 or wider, within the bound.
No kernel may reach another device: no remote copies, remote signals or barrier semaphores. Data moves between devices by JAX's collectives and lax.ppermute only.
A program may use at most 320 MiB of HBM per device.

v0:
```python
import jax
import jax.numpy as jnp
from jax import lax
from jax.sharding import PartitionSpec as P

D = 1024
EPS = 1e-05


def shifted(block, axis, distance):
    devices = range(lax.axis_size(axis))
    route = [(i - distance, i) for i in devices if i - distance in devices]
    return lax.ppermute(block, axis, route)


def dense(left, matrix, transposed):
    if transposed:
        return lax.dot_general(
            left, matrix, (((1,), (1,)), ((), ())), preferred_element_type=jnp.float32
        )
    return jnp.dot(left, matrix, preferred_element_type=jnp.float32)


def grads_of(left, right):
    return lax.dot_general(
        left, right, (((0,), (0,)), ((), ())), preferred_element_type=jnp.float32
    )


def tokens_by_row(value):
    return lax.all_gather(value, "row", axis=0, tiled=True)


def tokens_by_col(value):
    return lax.all_gather(value, "col", axis=0, tiled=True)


def spread_wide(gathered, matrix, transposed):
    height = gathered.shape[0] // lax.axis_size("col")

    def partial_rows(start, count):
        return dense(gathered, matrix, transposed)

    return lax.psum_scatter(
        partial_rows(jnp.int32(0), height * lax.axis_size("col")),
        "col",
        scatter_dimension=0,
        tiled=True,
    )


def spread_narrow(gathered, matrix, transposed):
    height = gathered.shape[0] // lax.axis_size("row")

    def partial_rows(start, count):
        return dense(gathered, matrix, transposed)

    return lax.psum_scatter(
        partial_rows(jnp.int32(0), height * lax.axis_size("row")),
        "row",
        scatter_dimension=0,
        tiled=True,
    )


def width_total(value):
    return lax.psum(value, "col")


def local(
    tokens,
    mixer_gain,
    in_weight,
    conv_kernel,
    out_weight,
    ffn_gain,
    ffn_weight,
    down_weight,
    cotangent,
):
    xfloat = tokens.astype(jnp.float32)
    scale_one = lax.rsqrt(width_total(jnp.sum(xfloat * xfloat, axis=1, keepdims=True)) / D + EPS)
    normed_one = xfloat * scale_one
    hidden_one = (normed_one * mixer_gain).astype(jnp.bfloat16)
    wide_in = in_weight.reshape(in_weight.shape[0], -1)
    gathered_one = tokens_by_row(hidden_one)
    projected = spread_wide(gathered_one, wide_in, False)
    block_width = conv_kernel.shape[1]
    gate_b = projected[:, :block_width]
    gate_c = projected[:, block_width : 2 * block_width]
    values = projected[:, 2 * block_width :]
    mixed_in = gate_b * values
    previous = shifted(mixed_in[-2:], "col", 1)
    extended = jnp.concatenate([previous, mixed_in], 0)
    lag_one = extended[1:-1]
    lag_two = extended[:-2]
    convolved = conv_kernel[2] * mixed_in + conv_kernel[1] * lag_one + conv_kernel[0] * lag_two
    mixer_out = (gate_c * convolved).astype(jnp.bfloat16)
    gathered_mix = tokens_by_col(mixer_out)
    residual = xfloat + spread_narrow(gathered_mix, out_weight, False)
    scale_two = lax.rsqrt(
        width_total(jnp.sum(residual * residual, axis=1, keepdims=True)) / D + EPS
    )
    normed_two = residual * scale_two
    hidden_two = (normed_two * ffn_gain).astype(jnp.bfloat16)
    wide_ffn = ffn_weight.reshape(ffn_weight.shape[0], -1)
    gathered_two = tokens_by_row(hidden_two)
    gate_up = spread_wide(gathered_two, wide_ffn, False)
    inner_width = down_weight.shape[0]
    gate_part = gate_up[:, :inner_width]
    up_part = gate_up[:, inner_width:]
    sigmoid_gate = jax.nn.sigmoid(gate_part)
    activated = (gate_part * sigmoid_gate * up_part).astype(jnp.bfloat16)
    gathered_act = tokens_by_col(activated)
    output = (residual + spread_narrow(gathered_act, down_weight, False)).astype(jnp.bfloat16)
    cot_rows = tokens_by_row(cotangent)
    d_act = spread_wide(cot_rows, down_weight, True)
    grad_down = grads_of(gathered_act, cot_rows)
    d_gate = d_act * up_part * sigmoid_gate * (1.0 + gate_part * (1.0 - sigmoid_gate))
    d_up = d_act * gate_part * sigmoid_gate
    d_gate_up = jnp.concatenate([d_gate, d_up], 1).astype(jnp.bfloat16)
    dgu_rows = tokens_by_col(d_gate_up)
    d_hidden_two = spread_narrow(dgu_rows, wide_ffn, True)
    grad_ffn = grads_of(gathered_two, dgu_rows).reshape(ffn_weight.shape)
    scaled_two = d_hidden_two * ffn_gain
    inner_two = width_total(jnp.sum(scaled_two * normed_two, axis=1, keepdims=True)) / D
    d_residual = cotangent.astype(jnp.float32) + scale_two * (scaled_two - normed_two * inner_two)
    gain_two_part = jnp.sum(d_hidden_two * normed_two, axis=0)
    d_residual_b = d_residual.astype(jnp.bfloat16)
    dres_rows = tokens_by_row(d_residual_b)
    d_mix = spread_wide(dres_rows, out_weight, True)
    grad_out = grads_of(gathered_mix, dres_rows)
    d_gate_c = d_mix * convolved
    d_conv = d_mix * gate_c
    following = shifted(d_conv[:2], "col", -1)
    ahead_rows = jnp.concatenate([d_conv, following], 0)
    d_mixed = (
        conv_kernel[2] * d_conv
        + conv_kernel[1] * ahead_rows[1:-1]
        + conv_kernel[0] * ahead_rows[2:]
    )
    kernel_part = jnp.stack(
        [
            jnp.sum(d_conv * lag_two, axis=0),
            jnp.sum(d_conv * lag_one, axis=0),
            jnp.sum(d_conv * mixed_in, axis=0),
        ]
    )
    d_projected = jnp.concatenate([d_mixed * values, d_gate_c, d_mixed * gate_b], 1).astype(
        jnp.bfloat16
    )
    dproj_rows = tokens_by_col(d_projected)
    d_hidden_one = spread_narrow(dproj_rows, wide_in, True)
    grad_in = grads_of(gathered_one, dproj_rows).reshape(in_weight.shape)
    scaled_one = d_hidden_one * mixer_gain
    inner_one = width_total(jnp.sum(scaled_one * normed_one, axis=1, keepdims=True)) / D
    d_tokens = d_residual + scale_one * (scaled_one - normed_one * inner_one)
    gain_one_part = jnp.sum(d_hidden_one * normed_one, axis=0)
    grad_in, grad_out, grad_ffn, grad_down = (
        lax.psum(grad_in.astype(jnp.bfloat16), "dp").astype(jnp.float32),
        lax.psum(grad_out.astype(jnp.bfloat16), "dp").astype(jnp.float32),
        lax.psum(grad_ffn.astype(jnp.bfloat16), "dp").astype(jnp.float32),
        lax.psum(grad_down.astype(jnp.bfloat16), "dp").astype(jnp.float32),
    )
    gain_width = mixer_gain.shape[0]
    col_offset = lax.axis_index("col") * gain_width
    row_offset = lax.axis_index("row") * block_width
    zero_index = jnp.zeros((), jnp.int32)
    full_one = lax.dynamic_update_slice(jnp.zeros((D,), jnp.float32), gain_one_part, (col_offset,))
    full_two = lax.dynamic_update_slice(jnp.zeros((D,), jnp.float32), gain_two_part, (col_offset,))
    full_kernel = lax.dynamic_update_slice(
        jnp.zeros((3, D), jnp.float32), kernel_part, (zero_index, row_offset)
    )
    total_one, total_two, total_kernel = lax.psum(
        (full_one, full_two, full_kernel), ("dp", "row", "col")
    )
    grad_gain_one = lax.dynamic_slice_in_dim(total_one, col_offset, gain_width, 0)
    grad_gain_two = lax.dynamic_slice_in_dim(total_two, col_offset, gain_width, 0)
    grad_kernel = lax.dynamic_slice_in_dim(total_kernel, row_offset, block_width, 1)
    return (
        output,
        d_tokens,
        grad_gain_one,
        grad_in,
        grad_kernel,
        grad_out,
        grad_gain_two,
        grad_ffn,
        grad_down,
    )


def solution(mesh):
    in_specs = (
        P(("dp", "row"), "col"),
        P("col"),
        P("col", None, "row"),
        P(None, "row"),
        P("row", "col"),
        P("col"),
        P("col", None, "row"),
        P("row", "col"),
        P(("dp", "row"), "col"),
    )
    out_specs = (
        P(("dp", "row"), "col"),
        P(("dp", "row"), "col"),
        P("col"),
        P("col", None, "row"),
        P(None, "row"),
        P("row", "col"),
        P("col"),
        P("col", None, "row"),
        P("row", "col"),
    )
    return jax.shard_map(local, mesh=mesh, in_specs=in_specs, out_specs=out_specs, check_vma=False)
```

profile of v0, /device:TPU:0, one launch (start us, length us, event | category | flops | bytes accessed | tf_op | source)
XLA Modules:
  0.0 1960.4 jit_solution(6422226700840039610)
XLA Ops:
  8.9 5.9 psum.77
  20.6 32.4 %all-gather.9.cloned.1.call-done = bf16[2048,512]{1,0:T(8,128)(2,1)} async-done(((bf16[1024,512]{1,0:T(8,128)(2,1)}), bf16[2048,512]{1,0:T(8,128)(2,1)}) %all-gather.9.cloned.1.call-update) | async-done | bytes 2097168 | tf_op jit(solution)/shard_map/all_gather | solution.py:31
  52.9 10.0 fusion.20
  63.1 144.6 %reduce-scatter.9.cloned.1.call-done = f32[1024,1536]{1,0:T(8,128)} async-done(((f32[2048,1536]{1,0:T(8,128)}), f32[1024,1536]{1,0:T(8,128)}) %reduce-scatter.9.cloned.1.call-update) | async-done | bytes 6291472 | tf_op jit(solution)/shard_map/reduce_scatter | solution.py:44
  218.1 35.1 %all-gather.11.cloned.1.call-done = bf16[2048,512]{1,0:T(8,128)(2,1)} async-done(((bf16[1024,512]{1,0:T(8,128)(2,1)}), bf16[2048,512]{1,0:T(8,128)(2,1)}) %all-gather.11.cloned.1.call-update) | async-done | bytes 2097168 | tf_op jit(solution)/shard_map/all_gather | solution.py:35
  258.8 53.9 %reduce-scatter.11.cloned.1.call-done = f32[1024,512]{1,0:T(8,128)} async-done(((f32[2048,512]{1,0:T(8,128)}), f32[1024,512]{1,0:T(8,128)}) %reduce-scatter.11.cloned.1.call-update) | async-done | bytes 2097168 | tf_op jit(solution)/shard_map/reduce_scatter | solution.py:58
  324.0 23.2 %all-gather.17.cloned.1.call-done = bf16[2048,512]{1,0:T(8,128)(2,1)} async-done(((bf16[1024,512]{1,0:T(8,128)(2,1)}), bf16[2048,512]{1,0:T(8,128)(2,1)}) %all-gather.17.cloned.1.call-update) | async-done | bytes 2097168 | tf_op jit(solution)/shard_map/all_gather | solution.py:31
  347.2 11.5 fusion.24
  364.6 17.7 all-gather.13.cloned.1.call-done
  382.3 20.5 %fusion.22 = f32[2048,4608]{1,0:T(8,128)} fusion(bf16[2048,512]{1,0:T(8,128)(2,1)} %all-gather.13.cloned.1.call-done, bf16[512,4608]{1,0:T(8,128)(2,1)} %bitcast.44), kind=kOutput, calls=%fused_computation.62 | convolution fusion | flops 9663676416 | bytes 44564480 | tf_op jit(solution)/shard_map/dot_general | solution.py:21
  402.9 193.5 %reduce-scatter.17.cloned.1.call-done = f32[1024,2304]{1,0:T(8,128)} async-done(((f32[2048,2304]{1,0:T(8,128)}), f32[1024,2304]{1,0:T(8,128)}) %reduce-scatter.17.cloned.1.call-update) | async-done | bytes 9437200 | tf_op jit(solution)/shard_map/reduce_scatter | solution.py:44
  596.4 416.3 %reduce-scatter.13.cloned.1.call-done = f32[1024,4608]{1,0:T(8,128)} async-done(((f32[2048,4608]{1,0:T(8,128)}), f32[1024,4608]{1,0:T(8,128)}) %reduce-scatter.13.cloned.1.call-update) | async-done | bytes 18874384 | tf_op jit(solution)/shard_map/reduce_scatter | solution.py:44
  1012.7 13.4 multiply_convert_fusion.1
  1030.8 224.4 %all-gather.19.cloned.1.call-done = bf16[2048,4608]{1,0:T(8,128)(2,1)} async-done(((bf16[1024,4608]{1,0:T(8,128)(2,1)}), bf16[2048,4608]{1,0:T(8,128)(2,1)}) %all-gather.19.cloned.1.call-update) | async-done | bytes 18874384 | tf_op jit(solution)/shard_map/all_gather | solution.py:35
  1255.2 16.5 fusion.25
  1271.8 54.5 %reduce-scatter.19.cloned.1.call-done = f32[1024,512]{1,0:T(8,128)} async-done(((f32[2048,512]{1,0:T(8,128)}), f32[1024,512]{1,0:T(8,128)}) %reduce-scatter.19.cloned.1.call-update) | async-done | bytes 2097168 | tf_op jit(solution)/shard_map/reduce_scatter | solution.py:58
  1337.9 33.2 %all-gather.21.cloned.1.call-done = bf16[2048,512]{1,0:T(8,128)(2,1)} async-done(((bf16[1024,512]{1,0:T(8,128)(2,1)}), bf16[2048,512]{1,0:T(8,128)(2,1)}) %all-gather.21.cloned.1.call-update) | async-done | bytes 2097168 | tf_op jit(solution)/shard_map/all_gather | solution.py:31
  1376.9 53.7 %reduce-scatter.21.cloned.1.call-done = f32[1024,512]{1,0:T(8,128)} async-done(((f32[2048,512]{1,0:T(8,128)}), f32[1024,512]{1,0:T(8,128)}) %reduce-scatter.21.cloned.1.call-update) | async-done | bytes 2097168 | tf_op jit(solution)/shard_map/reduce_scatter | solution.py:44
  1448.3 101.9 %all-gather.15.cloned.1.call-done = bf16[2048,2304]{1,0:T(8,128)(2,1)} async-done(((bf16[1024,2304]{1,0:T(8,128)(2,1)}), bf16[2048,2304]{1,0:T(8,128)(2,1)}) %all-gather.15.cloned.1.call-update) | async-done | bytes 9437200 | tf_op jit(solution)/shard_map/all_gather | solution.py:35
  1550.2 10.5 convolution_convert_fusion.1
  1560.7 16.5 convolution_convert_fusion
  1577.2 7.2 convert_element_type.70
  1588.7 43.9 %all-gather.23.cloned.1.call-done = bf16[2048,1536]{1,0:T(8,128)(2,1)} async-done(((bf16[1024,1536]{1,0:T(8,128)(2,1)}), bf16[2048,1536]{1,0:T(8,128)(2,1)}) %all-gather.23.cloned.1.call-update) | async-done | bytes 6291472 | tf_op jit(solution)/shard_map/all_gather | solution.py:35
  1632.5 8.0 convolution_convert_fusion.2
  1643.4 8.7 fusion.27
  1652.2 10.4 fusion.23
  1662.9 170.8 %all-reduce.4.cloned.1.call-done = (bf16[512,3,512]{0,2,1:T(8,128)(2,1)}, bf16[512,512]{1,0:T(8,128)(2,1)}, bf16[512,2,2304]{2,1,0:T(2,128)(2,1)}, bf16[2304,512]{1,0:T(8,128)(2,1)}) async-done(((bf16[512,3,512]{0,2,1:T(8,128)(2,1)}, bf16[512,512]{1,0:T(8,128)(2,1)}, bf16[512,2,2304]{2,1,0:T(2,128)(2,1)}, bf16[2304,512]{1,0:T(8,128)(2,1)}), (bf16[512,3,512]{0,2,1:T(8,128)(2,1)}, bf16[512,512]{1,0:T(8,128)(2,1)}, ...) | async-done | bytes 9175056 | tf_op jit(solution)/shard_map/psum | solution.py:160
  1833.7 7.4 convert_element_type.71
  1849.3 41.1 %reduce-scatter.23.cloned.1.call-done = f32[1024,512]{1,0:T(8,128)} async-done(((f32[2048,512]{1,0:T(8,128)}), f32[1024,512]{1,0:T(8,128)}) %reduce-scatter.23.cloned.1.call-update) | async-done | bytes 2097168 | tf_op jit(solution)/shard_map/reduce_scatter | solution.py:58
  1892.9 40.3 %all-reduce = (f32[1024]{0:T(1024)S(1)}, f32[3,1024]{1,0:T(4,128)S(1)}, f32[1024]{0:T(1024)S(1)}) all-reduce(f32[1024]{0:T(1024)S(1)} %dynamic_update_slice.9, f32[3,1024]{1,0:T(4,128)S(1)} %maximum_dynamic-update-slice_fusion, f32[1024]{0:T(1024)S(1)} %dynamic_update_slice.11), channel_id=1, replica_groups=mesh['dp'=8,'row'=2,'col'=2] {'dp','row','col'}, use_global_device_ids=true, to_apply=%region_17.0 | all-reduce | flops 5120 | bytes 40960 | tf_op jit(solution)/shard_map/psum | solution.py:174
  1940.3 7.9 reduce-scatter.15.cloned.1.call-done
  1948.2 5.5 fusion.13
  (106 shorter events, 105.4 us)
Async XLA Ops:
  7.2 340.0 %copy-start = (bf16[2304,512]{1,0:T(8,128)(2,1)S(1)}, bf16[2304,512]{1,0:T(8,128)(2,1)}, u32[]{:S(2)}) copy-start(bf16[2304,512]{1,0:T(8,128)(2,1)} %param.16) | copy-start | bytes 7077892
  7.2 45.8 %all-gather.9.cloned.1.call-start = ((), (), s32[]{:S(2)}) async-start(), calls=%async_computation.8 | async-start | bytes 3145728 | tf_op jit(solution)/shard_map/all_gather | solution.py:31
  14.8 0.6 copy-start.7
  17.9 189.8 %reduce-scatter.9.cloned.1.call-start = ((), (), s32[]{:S(2)}) async-start(), calls=%async_computation.9 | async-start | bytes 18874368 | tf_op jit(solution)/shard_map/reduce_scatter | solution.py:44
  63.0 149.7 %copy-start.11 = (f32[3,512]{1,0:T(4,128)S(1)}, f32[3,512]{1,0:T(4,128)}, u32[]{:S(2)}) copy-start(f32[3,512]{1,0:T(4,128)} %param.12) | copy-start | bytes 18436
  63.0 190.3 %all-gather.11.cloned.1.call-start = ((), (), s32[]{:S(2)}) async-start(), calls=%async_computation.10 | async-start | bytes 3145728 | tf_op jit(solution)/shard_map/all_gather | solution.py:35
  210.4 7.7 copy-start.3
  210.4 3.6 collective-permute-start
  214.0 39.3 %copy-start.6 = (bf16[512,512]{1,0:T(8,128)(2,1)S(1)}, bf16[512,512]{1,0:T(8,128)(2,1)}, u32[]{:S(2)}) copy-start(bf16[512,512]{1,0:T(8,128)(2,1)} %param.13) | copy-start | bytes 1572868
  218.1 94.6 %reduce-scatter.11.cloned.1.call-start = ((), (), s32[]{:S(2)}) async-start(), calls=%async_computation.11 | async-start | bytes 6291456 | tf_op jit(solution)/shard_map/reduce_scatter | solution.py:58
  258.1 54.6 %copy-start.1 = (bf16[1024,512]{1,0:T(8,128)(2,1)S(1)}, bf16[1024,512]{1,0:T(8,128)(2,1)}, u32[]{:S(2)}) copy-start(bf16[1024,512]{1,0:T(8,128)(2,1)} %param.9) | copy-start | bytes 3145732
  258.2 89.0 %all-gather.17.cloned.1.call-start = ((), (), s32[]{:S(2)}) async-start(), calls=%async_computation.16 | async-start | bytes 3145728 | tf_op jit(solution)/shard_map/all_gather | solution.py:31
  258.7 62.1 %copy-start.9 = (f32[512]{0:T(512)S(1)}, f32[512]{0:T(512)}, u32[]{:S(2)}) copy-start(f32[512]{0:T(512)} %param.14) | copy-start | bytes 6148
  258.8 123.5 %all-gather.13.cloned.1.call-start = ((), (), s32[]{:S(2)}) async-start(), calls=%async_computation.12 | async-start | bytes 3145728 | tf_op jit(solution)/shard_map/all_gather | solution.py:31
  323.9 272.5 %reduce-scatter.17.cloned.1.call-start = ((), (), s32[]{:S(2)}) async-start(), calls=%async_computation.17 | async-start | bytes 28311552 | tf_op jit(solution)/shard_map/reduce_scatter | solution.py:44
  358.8 653.9 %reduce-scatter.13.cloned.1.call-start = ((), (), s32[]{:S(2)}) async-start(), calls=%async_computation.13 | async-start | bytes 56623104 | tf_op jit(solution)/shard_map/reduce_scatter | solution.py:44
  402.8 852.4 %all-gather.19.cloned.1.call-start = ((), (), s32[]{:S(2)}) async-start(), calls=%async_computation.18 | async-start | bytes 28311552 | tf_op jit(solution)/shard_map/all_gather | solution.py:35
  1030.7 295.5 %reduce-scatter.19.cloned.1.call-start = ((), (), s32[]{:S(2)}) async-start(), calls=%async_computation.19 | async-start | bytes 6291456 | tf_op jit(solution)/shard_map/reduce_scatter | solution.py:58
  1271.7 62.3 %copy-start.4 = (bf16[1024,512]{1,0:T(8,128)(2,1)S(1)}, bf16[1024,512]{1,0:T(8,128)(2,1)}, u32[]{:S(2)}) copy-start(bf16[1024,512]{1,0:T(8,128)(2,1)} %param.17) | copy-start | bytes 3145732
  1271.7 99.4 %all-gather.21.cloned.1.call-start = ((), (), s32[]{:S(2)}) async-start(), calls=%async_computation.20 | async-start | bytes 3145728 | tf_op jit(solution)/shard_map/all_gather | solution.py:31
  1337.8 92.8 %reduce-scatter.21.cloned.1.call-start = ((), (), s32[]{:S(2)}) async-start(), calls=%async_computation.21 | async-start | bytes 6291456 | tf_op jit(solution)/shard_map/reduce_scatter | solution.py:44
  1376.1 174.1 %all-gather.15.cloned.1.call-start = ((), (), s32[]{:S(2)}) async-start(), calls=%async_computation.14 | async-start | bytes 14155776 | tf_op jit(solution)/shard_map/all_gather | solution.py:35
  1376.8 255.7 %all-gather.23.cloned.1.call-start = ((), (), s32[]{:S(2)}) async-start(), calls=%async_computation.22 | async-start | bytes 9437184 | tf_op jit(solution)/shard_map/all_gather | solution.py:35
  1435.9 5.5 collective-permute-start.1
  1448.3 385.5 %all-reduce.4.cloned.1.call-start = ((), (), s32[]{:S(2)}) async-start(), calls=%async_computation.24 | async-start | bytes 18350080 | tf_op jit(solution)/shard_map/psum | solution.py:160
  1550.2 10.5 copy-start.12
  1643.2 247.2 %reduce-scatter.23.cloned.1.call-start = ((), (), s32[]{:S(2)}) async-start(), calls=%async_computation.23 | async-start | bytes 6291456 | tf_op jit(solution)/shard_map/reduce_scatter | solution.py:58
  1652.2 296.0 %reduce-scatter.15.cloned.1.call-start = ((), (), s32[]{:S(2)}) async-start(), calls=%async_computation.15 | async-start | bytes 6291456 | tf_op jit(solution)/shard_map/reduce_scatter | solution.py:58
  1833.7 7.4 copy-start.5
  1844.0 46.4 %copy-start.2 = (bf16[1024,512]{1,0:T(8,128)(2,1)S(1)}, bf16[1024,512]{1,0:T(8,128)(2,1)}, u32[]{:S(2)}) copy-start(bf16[1024,512]{1,0:T(8,128)(2,1)} %param.9) | copy-start | bytes 3145732
  1844.0 46.4 %copy-start.8 = (f32[1024,1]{0,1:T(1,128)S(1)}, f32[1024,1]{0,1:T(1,128)}, u32[]{:S(2)}) copy-start(f32[1024,1]{0,1:T(1,128)} %copy-done.7) | copy-start | bytes 12292
  1844.0 46.4 %copy-start.10 = (f32[512]{0:T(512)S(1)}, f32[512]{0:T(512)}, u32[]{:S(2)}) copy-start(f32[512]{0:T(512)} %param.10) | copy-start | bytes 6148
Sparse Core Ops, SparseCore 0:
  18.1 34.8 all-gather.8
  63.1 144.5 reduce-scatter.8
  218.2 35.0 all-gather.10
  258.3 54.3 reduce-scatter.10
  314.1 33.0 all-gather.16
  349.2 33.0 all-gather.12
  384.6 211.7 reduce-scatter.16
  598.7 413.9 reduce-scatter.12
  1030.9 224.3 all-gather.18
  1271.8 54.3 reduce-scatter.18
  1337.9 33.0 all-gather.20
  1376.2 54.3 reduce-scatter.20
  1432.2 117.9 all-gather.14
  1552.2 80.3 all-gather.22
  1643.3 190.3 all-reduce.3
  1835.9 54.4 reduce-scatter.22
  1892.6 55.5 reduce-scatter.14
where the time goes:
time: 1970 us; the launch traced here: 1960 us
  waiting for transfers between devices  1660 us (84%)
  matrix products  127 us (6%)
  other arithmetic  74.1 us (4%)
  blocking collectives  61.2 us (3%)
  local copies, waits for them, and re-layouts  23.9 us (1%)
    reduce_scatter x4, waiting for transfers between devices, spread_wide(): lax.psum_scatter(partial_rows(jnp.int32(0), height * lax.axis_size('col')...  808 us
    all_gather x4, waiting for transfers between devices, tokens_by_col(): return lax.all_gather(value, 'col', axis=0, tiled=True)  405 us
    psum x1, waiting for transfers between devices, local(): lax.psum(grad_in.astype(jnp.bfloat16), 'dp').astype(jnp.float32)  171 us
    reduce_scatter x4, waiting for transfers between devices, spread_narrow(): lax.psum_scatter(partial_rows(jnp.int32(0), height * lax.axis_size('row')...  157 us
    all_gather x4, waiting for transfers between devices, tokens_by_row(): return lax.all_gather(value, 'row', axis=0, tiled=True)  107 us
    dot_general x4, matrix products, dense(): return jnp.dot(left, matrix, preferred_element_type=jnp.float32)  45.8 us
    dot_general x4, matrix products, dense(): lax.dot_general(left, matrix, (((1,), (1,)), ((), ())), preferred_element...  41.7 us
    psum x1, blocking collectives, local(): lax.psum((full_one, full_two, full_kernel), ('dp', 'row', 'col'))  40.3 us
  transfers between devices with their start and end apart: 19, of which 19 were waited for; matrix products, arithmetic and copies ran while one was open for 7% of the time, Pallas kernels for 0%

commit v1 on v0

--- a/solution.py
+++ b/solution.py
@@ -157,7 +157,7 @@
     d_tokens = d_residual + scale_one * (scaled_one - normed_one * inner_one)
     gain_one_part = jnp.sum(d_hidden_one * normed_one, axis=0)
     grad_in, grad_out, grad_ffn, grad_down = (
-        lax.psum(grad_in.astype(jnp.bfloat16), "dp").astype(jnp.float32),
+        jnp.sum(lax.all_gather(grad_in.astype(jnp.bfloat16), "dp"), axis=0).astype(jnp.float32),
         lax.psum(grad_out.astype(jnp.bfloat16), "dp").astype(jnp.float32),
         lax.psum(grad_ffn.astype(jnp.bfloat16), "dp").astype(jnp.float32),
         lax.psum(grad_down.astype(jnp.bfloat16), "dp").astype(jnp.float32),

time: 1970 us -> 2060 us (1.046)
  waiting for transfers between devices: 1660 us -> 1730 us
    all_gather x0 -> x1, waiting for transfers between devices: none -> 113 us  [local(): lax.all_gather(grad_in.astype(jnp.bfloat16), 'dp')]
    psum x1, waiting for transfers between devices: 171 us -> 131 us  [local(): lax.psum(grad_out.astype(jnp.bfloat16), 'dp').astype(jnp.float32)]
  transfers between devices with their start and end apart: 19 -> 20, of which waited for: 19 -> 20; matrix products, arithmetic and copies ran while one was open for 7% -> 7% of each run, Pallas kernels for 0% -> 0%
where the time goes in v1:
time: 2060 us; the launch traced here: 2050 us
  waiting for transfers between devices  1730 us (84%)
  matrix products  127 us (6%)
  other arithmetic  80.9 us (4%)
  blocking collectives  61.5 us (3%)
  local copies, waits for them, and re-layouts  29 us (1%)
    reduce_scatter x4, waiting for transfers between devices, spread_wide(): lax.psum_scatter(partial_rows(jnp.int32(0), height * lax.axis_size('col')...  808 us
    all_gather x4, waiting for transfers between devices, tokens_by_col(): return lax.all_gather(value, 'col', axis=0, tiled=True)  405 us
    reduce_scatter x4, waiting for transfers between devices, spread_narrow(): lax.psum_scatter(partial_rows(jnp.int32(0), height * lax.axis_size('row')...  161 us
    psum x1, waiting for transfers between devices, local(): lax.psum(grad_out.astype(jnp.bfloat16), 'dp').astype(jnp.float32)  131 us
    all_gather x1, waiting for transfers between devices, local(): lax.all_gather(grad_in.astype(jnp.bfloat16), 'dp')  113 us
    all_gather x4, waiting for transfers between devices, tokens_by_row(): return lax.all_gather(value, 'row', axis=0, tiled=True)  107 us
    dot_general x4, matrix products, dense(): return jnp.dot(left, matrix, preferred_element_type=jnp.float32)  45.9 us
    dot_general x4, matrix products, dense(): lax.dot_general(left, matrix, (((1,), (1,)), ((), ())), preferred_element...  41.7 us
  transfers between devices with their start and end apart: 20, of which 20 were waited for; matrix products, arithmetic and copies ran while one was open for 7% of the time, Pallas kernels for 0%

profile of v1, /device:TPU:0, one launch (start us, length us, event | category | flops | bytes accessed | tf_op | source)
XLA Modules:
  0.0 2049.5 jit_solution(395635068826477682)
XLA Ops:
  20.6 32.4 %all-gather.10.cloned.1.call-done = bf16[2048,512]{1,0:T(8,128)(2,1)} async-done(((bf16[1024,512]{1,0:T(8,128)(2,1)}), bf16[2048,512]{1,0:T(8,128)(2,1)}) %all-gather.10.cloned.1.call-update) | async-done | bytes 2097168 | tf_op jit(solution)/shard_map/all_gather | solution.py:31
  52.9 10.0 fusion.20
  63.1 144.6 %reduce-scatter.9.cloned.1.call-done = f32[1024,1536]{1,0:T(8,128)} async-done(((f32[2048,1536]{1,0:T(8,128)}), f32[1024,1536]{1,0:T(8,128)}) %reduce-scatter.9.cloned.1.call-update) | async-done | bytes 6291472 | tf_op jit(solution)/shard_map/reduce_scatter | solution.py:44
  218.2 35.1 %all-gather.12.cloned.1.call-done = bf16[2048,512]{1,0:T(8,128)(2,1)} async-done(((bf16[1024,512]{1,0:T(8,128)(2,1)}), bf16[2048,512]{1,0:T(8,128)(2,1)}) %all-gather.12.cloned.1.call-update) | async-done | bytes 2097168 | tf_op jit(solution)/shard_map/all_gather | solution.py:35
  258.8 53.9 %reduce-scatter.11.cloned.1.call-done = f32[1024,512]{1,0:T(8,128)} async-done(((f32[2048,512]{1,0:T(8,128)}), f32[1024,512]{1,0:T(8,128)}) %reduce-scatter.11.cloned.1.call-update) | async-done | bytes 2097168 | tf_op jit(solution)/shard_map/reduce_scatter | solution.py:58
  324.0 23.2 %all-gather.18.cloned.1.call-done = bf16[2048,512]{1,0:T(8,128)(2,1)} async-done(((bf16[1024,512]{1,0:T(8,128)(2,1)}), bf16[2048,512]{1,0:T(8,128)(2,1)}) %all-gather.18.cloned.1.call-update) | async-done | bytes 2097168 | tf_op jit(solution)/shard_map/all_gather | solution.py:31
  347.2 11.5 fusion.24
  364.3 18.0 all-gather.14.cloned.1.call-done
  382.3 20.5 fusion.22
  402.9 193.5 %reduce-scatter.17.cloned.1.call-done = f32[1024,2304]{1,0:T(8,128)} async-done(((f32[2048,2304]{1,0:T(8,128)}), f32[1024,2304]{1,0:T(8,128)}) %reduce-scatter.17.cloned.1.call-update) | async-done | bytes 9437200 | tf_op jit(solution)/shard_map/reduce_scatter | solution.py:44
  596.4 416.3 %reduce-scatter.13.cloned.1.call-done = f32[1024,4608]{1,0:T(8,128)} async-done(((f32[2048,4608]{1,0:T(8,128)}), f32[1024,4608]{1,0:T(8,128)}) %reduce-scatter.13.cloned.1.call-update) | async-done | bytes 18874384 | tf_op jit(solution)/shard_map/reduce_scatter | solution.py:44
  1012.7 13.4 multiply_convert_fusion.1
  1030.8 224.4 %all-gather.20.cloned.1.call-done = bf16[2048,4608]{1,0:T(8,128)(2,1)} async-done(((bf16[1024,4608]{1,0:T(8,128)(2,1)}), bf16[2048,4608]{1,0:T(8,128)(2,1)}) %all-gather.20.cloned.1.call-update) | async-done | bytes 18874384 | tf_op jit(solution)/shard_map/all_gather | solution.py:35
  1255.2 16.5 fusion.25
  1271.8 54.5 %reduce-scatter.19.cloned.1.call-done = f32[1024,512]{1,0:T(8,128)} async-done(((f32[2048,512]{1,0:T(8,128)}), f32[1024,512]{1,0:T(8,128)}) %reduce-scatter.19.cloned.1.call-update) | async-done | bytes 2097168 | tf_op jit(solution)/shard_map/reduce_scatter | solution.py:58
  1337.9 33.2 %all-gather.22.cloned.1.call-done = bf16[2048,512]{1,0:T(8,128)(2,1)} async-done(((bf16[1024,512]{1,0:T(8,128)(2,1)}), bf16[2048,512]{1,0:T(8,128)(2,1)}) %all-gather.22.cloned.1.call-update) | async-done | bytes 2097168 | tf_op jit(solution)/shard_map/all_gather | solution.py:31
  1376.9 53.7 %reduce-scatter.21.cloned.1.call-done = f32[1024,512]{1,0:T(8,128)} async-done(((f32[2048,512]{1,0:T(8,128)}), f32[1024,512]{1,0:T(8,128)}) %reduce-scatter.21.cloned.1.call-update) | async-done | bytes 2097168 | tf_op jit(solution)/shard_map/reduce_scatter | solution.py:44
  1448.2 101.9 %all-gather.16.cloned.1.call-done = bf16[2048,2304]{1,0:T(8,128)(2,1)} async-done(((bf16[1024,2304]{1,0:T(8,128)(2,1)}), bf16[2048,2304]{1,0:T(8,128)(2,1)}) %all-gather.16.cloned.1.call-update) | async-done | bytes 9437200 | tf_op jit(solution)/shard_map/all_gather | solution.py:35
  1550.2 10.6 convolution_convert_fusion.1
  1560.8 16.5 convolution_convert_fusion
  1577.2 7.2 convert_element_type.79
  1589.2 43.4 %all-gather.24.cloned.1.call-done = bf16[2048,1536]{1,0:T(8,128)(2,1)} async-done(((bf16[1024,1536]{1,0:T(8,128)(2,1)}), bf16[2048,1536]{1,0:T(8,128)(2,1)}) %all-gather.24.cloned.1.call-update) | async-done | bytes 6291472 | tf_op jit(solution)/shard_map/all_gather | solution.py:35
  1632.5 8.7 fusion.27
  1641.4 10.5 fusion.23
  1651.9 8.1 convolution_convert_fusion.2
  1665.5 130.9 %all-reduce.4.cloned.1.call-done = (bf16[512,512]{1,0:T(8,128)(2,1)}, bf16[512,2,2304]{2,1,0:T(2,128)(2,1)}, bf16[2304,512]{1,0:T(8,128)(2,1)}) async-done(((bf16[512,512]{1,0:T(8,128)(2,1)}, bf16[512,2,2304]{2,1,0:T(2,128)(2,1)}, bf16[2304,512]{1,0:T(8,128)(2,1)}), (bf16[512,512]{1,0:T(8,128)(2,1)}, bf16[512,2,2304]{2,1,0:T(2,128)(2,1)}, bf16[2304,512]{1,0:T(8,128)(2,1)})) %all-reduce.4.cloned.1.call-update) | async-done | bytes 7602192 | tf_op jit(solution)/shard_map/psum | solution.py:161
  1796.4 7.4 convert_element_type.80
  1807.7 45.3 %reduce-scatter.23.cloned.1.call-done = f32[1024,512]{1,0:T(8,128)} async-done(((f32[2048,512]{1,0:T(8,128)}), f32[1024,512]{1,0:T(8,128)}) %reduce-scatter.23.cloned.1.call-update) | async-done | bytes 2097168 | tf_op jit(solution)/shard_map/reduce_scatter | solution.py:58
  1855.5 40.4 %all-reduce = (f32[1024]{0:T(1024)S(1)}, f32[3,1024]{1,0:T(4,128)S(1)}, f32[1024]{0:T(1024)S(1)}) all-reduce(f32[1024]{0:T(1024)S(1)} %dynamic_update_slice.9, f32[3,1024]{1,0:T(4,128)S(1)} %maximum_dynamic-update-slice_fusion, f32[1024]{0:T(1024)S(1)} %dynamic_update_slice.11), channel_id=1, replica_groups=mesh['dp'=8,'row'=2,'col'=2] {'dp','row','col'}, use_global_device_ids=true, to_apply=%region_17.0 | all-reduce | flops 5120 | bytes 40960 | tf_op jit(solution)/shard_map/psum | solution.py:174
  1903.2 7.6 reduce-scatter.15.cloned.1.call-done
  1916.3 112.6 %all-gather.26.cloned.1.call-done = bf16[8,512,3,512]{3,1,2,0:T(8,128)(2,1)} async-done(((bf16[1,512,3,512]{3,1,2,0:T(8,128)(2,1)}), bf16[8,512,3,512]{3,1,2,0:T(8,128)(2,1)}) %all-gather.26.cloned.1.call-update) | async-done | bytes 12582928 | tf_op jit(solution)/shard_map/all_gather | solution.py:160
  2028.8 8.0 reduce_sum.98
  (114 shorter events, 120.9 us)
Async XLA Ops:
  7.2 340.0 %copy-start = (bf16[2304,512]{1,0:T(8,128)(2,1)S(1)}, bf16[2304,512]{1,0:T(8,128)(2,1)}, u32[]{:S(2)}) copy-start(bf16[2304,512]{1,0:T(8,128)(2,1)} %param.16) | copy-start | bytes 7077892
  7.2 45.8 %all-gather.10.cloned.1.call-start = ((), (), s32[]{:S(2)}) async-start(), calls=%async_computation.8 | async-start | bytes 3145728 | tf_op jit(solution)/shard_map/all_gather | solution.py:31
  17.9 189.8 %reduce-scatter.9.cloned.1.call-start = ((), (), s32[]{:S(2)}) async-start(), calls=%async_computation.9 | async-start | bytes 18874368 | tf_op jit(solution)/shard_map/reduce_scatter | solution.py:44
  63.0 149.7 %copy-start.12 = (f32[3,512]{1,0:T(4,128)S(1)}, f32[3,512]{1,0:T(4,128)}, u32[]{:S(2)}) copy-start(f32[3,512]{1,0:T(4,128)} %param.12) | copy-start | bytes 18436
  63.0 190.3 %all-gather.12.cloned.1.call-start = ((), (), s32[]{:S(2)}) async-start(), calls=%async_computation.10 | async-start | bytes 3145728 | tf_op jit(solution)/shard_map/all_gather | solution.py:35
  210.4 7.7 copy-start.3
  210.4 3.6 collective-permute-start
  214.0 39.3 %copy-start.6 = (bf16[512,512]{1,0:T(8,128)(2,1)S(1)}, bf16[512,512]{1,0:T(8,128)(2,1)}, u32[]{:S(2)}) copy-start(bf16[512,512]{1,0:T(8,128)(2,1)} %param.13) | copy-start | bytes 1572868
  218.1 94.6 %reduce-scatter.11.cloned.1.call-start = ((), (), s32[]{:S(2)}) async-start(), calls=%async_computation.11 | async-start | bytes 6291456 | tf_op jit(solution)/shard_map/reduce_scatter | solution.py:58
  258.1 54.6 %copy-start.1 = (bf16[1024,512]{1,0:T(8,128)(2,1)S(1)}, bf16[1024,512]{1,0:T(8,128)(2,1)}, u32[]{:S(2)}) copy-start(bf16[1024,512]{1,0:T(8,128)(2,1)} %param.9) | copy-start | bytes 3145732
  258.2 89.1 %all-gather.18.cloned.1.call-start = ((), (), s32[]{:S(2)}) async-start(), calls=%async_computation.16 | async-start | bytes 3145728 | tf_op jit(solution)/shard_map/all_gather | solution.py:31
  258.7 62.1 %copy-start.10 = (f32[512]{0:T(512)S(1)}, f32[512]{0:T(512)}, u32[]{:S(2)}) copy-start(f32[512]{0:T(512)} %param.14) | copy-start | bytes 6148
  258.8 123.6 %all-gather.14.cloned.1.call-start = ((), (), s32[]{:S(2)}) async-start(), calls=%async_computation.12 | async-start | bytes 3145728 | tf_op jit(solution)/shard_map/all_gather | solution.py:31
  323.9 272.5 %reduce-scatter.17.cloned.1.call-start = ((), (), s32[]{:S(2)}) async-start(), calls=%async_computation.17 | async-start | bytes 28311552 | tf_op jit(solution)/shard_map/reduce_scatter | solution.py:44
  358.8 653.9 %reduce-scatter.13.cloned.1.call-start = ((), (), s32[]{:S(2)}) async-start(), calls=%async_computation.13 | async-start | bytes 56623104 | tf_op jit(solution)/shard_map/reduce_scatter | solution.py:44
  402.8 852.4 %all-gather.20.cloned.1.call-start = ((), (), s32[]{:S(2)}) async-start(), calls=%async_computation.18 | async-start | bytes 28311552 | tf_op jit(solution)/shard_map/all_gather | solution.py:35
  1030.7 295.5 %reduce-scatter.19.cloned.1.call-start = ((), (), s32[]{:S(2)}) async-start(), calls=%async_computation.19 | async-start | bytes 6291456 | tf_op jit(solution)/shard_map/reduce_scatter | solution.py:58
  1271.7 62.3 %copy-start.4 = (bf16[1024,512]{1,0:T(8,128)(2,1)S(1)}, bf16[1024,512]{1,0:T(8,128)(2,1)}, u32[]{:S(2)}) copy-start(bf16[1024,512]{1,0:T(8,128)(2,1)} %param.17) | copy-start | bytes 3145732
  1271.7 99.4 %all-gather.22.cloned.1.call-start = ((), (), s32[]{:S(2)}) async-start(), calls=%async_computation.20 | async-start | bytes 3145728 | tf_op jit(solution)/shard_map/all_gather | solution.py:31
  1337.8 92.8 %reduce-scatter.21.cloned.1.call-start = ((), (), s32[]{:S(2)}) async-start(), calls=%async_computation.21 | async-start | bytes 6291456 | tf_op jit(solution)/shard_map/reduce_scatter | solution.py:44
  1376.1 174.1 %all-gather.16.cloned.1.call-start = ((), (), s32[]{:S(2)}) async-start(), calls=%async_computation.14 | async-start | bytes 14155776 | tf_op jit(solution)/shard_map/all_gather | solution.py:35
  1376.8 255.7 %all-gather.24.cloned.1.call-start = ((), (), s32[]{:S(2)}) async-start(), calls=%async_computation.22 | async-start | bytes 9437184 | tf_op jit(solution)/shard_map/all_gather | solution.py:35
  1435.8 5.5 collective-permute-start.1
  1448.2 348.2 %all-reduce.4.cloned.1.call-start = ((), (), s32[]{:S(2)}) async-start(), calls=%async_computation.25 | async-start | bytes 15204352 | tf_op jit(solution)/shard_map/psum | solution.py:161
  1550.2 10.6 copy-start.13
  1588.7 264.3 %reduce-scatter.23.cloned.1.call-start = ((), (), s32[]{:S(2)}) async-start(), calls=%async_computation.23 | async-start | bytes 6291456 | tf_op jit(solution)/shard_map/reduce_scatter | solution.py:58
  1641.3 269.5 %reduce-scatter.15.cloned.1.call-start = ((), (), s32[]{:S(2)}) async-start(), calls=%async_computation.15 | async-start | bytes 6291456 | tf_op jit(solution)/shard_map/reduce_scatter | solution.py:58
  1651.9 377.0 %all-gather.26.cloned.1.call-start = ((), (), s32[]{:S(2)}) async-start(), calls=%async_computation.24 | async-start | bytes 14155776 | tf_op jit(solution)/shard_map/all_gather | solution.py:160
  1796.4 7.4 copy-start.5
  1803.7 49.3 %copy-start.9 = (f32[1024,1]{0,1:T(1,128)S(1)}, f32[1024,1]{0,1:T(1,128)}, u32[]{:S(2)}) copy-start(f32[1024,1]{0,1:T(1,128)} %copy-done.8) | copy-start | bytes 12292
  1803.8 49.3 %copy-start.11 = (f32[512]{0:T(512)S(1)}, f32[512]{0:T(512)}, u32[]{:S(2)}) copy-start(f32[512]{0:T(512)} %param.10) | copy-start | bytes 6148
  1806.6 46.4 %copy-start.2 = (bf16[1024,512]{1,0:T(8,128)(2,1)S(1)}, bf16[1024,512]{1,0:T(8,128)(2,1)}, u32[]{:S(2)}) copy-start(bf16[1024,512]{1,0:T(8,128)(2,1)} %param.9) | copy-start | bytes 3145732
  (2 other events, 3.5 us)
Sparse Core Ops, SparseCore 0:
  18.1 34.8 all-gather.9
  63.1 144.5 reduce-scatter.8
  218.2 35.0 all-gather.11
  258.3 54.3 reduce-scatter.10
  314.1 33.0 all-gather.17
  349.2 33.0 all-gather.13
  384.6 211.7 reduce-scatter.16
  598.7 413.9 reduce-scatter.12
  1030.9 224.3 all-gather.19
  1271.8 54.3 reduce-scatter.18
  1337.9 33.0 all-gather.21
  1376.2 54.3 reduce-scatter.20
  1432.2 117.9 all-gather.15
  1552.2 80.3 all-gather.23
  1635.6 160.7 all-reduce.3
  1798.5 54.4 reduce-scatter.22
  1855.1 55.5 reduce-scatter.14
  1912.3 116.5 all-gather.25
